TPU v7x, 256 devices: a whole 4x4x8 slice. The times are simulated.
256 devices in a mesh: row: 32 (over x, y, z_lo), src: 8 (over z_hi, core).
Axes of the slice: x: 4, y: 4, z: 8 (z_hi: 4, z_lo: 2; z = z_hi * 2 + z_lo), core: 2. Of those that a mesh axis runs over, the one named last changes fastest.
Arguments:
- traces: bfloat16 [16384, 128, 512], P('row', 'src'), may hold values from -6 to 6
- row_source: int32 [16384], P('row'), may hold values from 0 to 16383, as said below
- slice_data: bfloat16 [2, 16384, 32, 512], P(None, 'row', None, 'src'), may hold values from -0.03125 to 0.03125
- wavelet_inverse: float32 [2], replicated, may hold values from 0.3 to 0.8
Outputs:
- multiples: float32 [16384, 2, 128], P(('row', 'src'))
- primaries: float32 [16384, 2, 128], P(('row', 'src'))
Inputs may be any that keep to these rules, and one draw needn't show every extreme that they name: `row_source`: every recording row is named exactly once; entry e * 512 + p names a recording row whose index modulo 512 lies in [e * 16, (e + 1) * 16).
All inputs are finite; a program needn't handle non-finite values.
Results may differ from a plain program's by a relative error of at most 0.0056.
Values may be sent and summed in bfloat16 or wider, within the bound.
A program may use at most 64 MiB of HBM per device.

v0:
```python
import jax
import jax.numpy as jnp
from jax import lax
from jax.sharding import PartitionSpec as P

FREQ = 61
ITERS = 3


def dft_kernel(samples):
    ticks = jnp.arange(samples, dtype=jnp.int32)
    moment = ticks.astype(jnp.float32)
    ramp_len = samples // 8
    rising = 0.5 - 0.5 * jnp.cos(jnp.pi * (moment + 0.5) / ramp_len)
    falling = 0.5 - 0.5 * jnp.cos(jnp.pi * (samples - moment - 0.5) / ramp_len)
    taper = jnp.where(
        ticks < ramp_len,
        rising,
        jnp.where(ticks >= samples - ramp_len, falling, jnp.ones_like(rising)),
    )
    wrapped = ticks * FREQ % samples
    angles = 2.0 * jnp.pi / samples * wrapped.astype(jnp.float32)
    factor = 1.0 / jnp.sqrt(jnp.float32(samples))
    table = jnp.stack([taper * jnp.cos(angles) * factor, -taper * jnp.sin(angles) * factor], axis=1)
    return table.astype(jnp.bfloat16)


def combine_parts(real_terms, imag_terms, shot_count):
    pred_real = real_terms[:, :shot_count] - imag_terms[:, shot_count:]
    pred_imag = real_terms[:, shot_count:] + imag_terms[:, :shot_count]
    return jnp.stack([pred_real, pred_imag], axis=1)


def body(traces, row_source, slice_data, wavelet_inverse):
    block_rows, shot_local, samples = traces.shape
    kernel = dft_kernel(samples)
    spectra = jnp.dot(
        traces.reshape(block_rows * shot_local, samples), kernel, preferred_element_type=jnp.float32
    )
    spectra = jnp.transpose(spectra.reshape(block_rows, shot_local, 2), (0, 2, 1)).astype(
        jnp.bfloat16
    )
    arrived = lax.all_to_all(spectra, "row", split_axis=0, concat_axis=0, tiled=True)
    group_rows = block_rows // lax.axis_size("row")
    located = row_source // block_rows * group_rows + row_source % group_rows
    ordered = arrived[located]
    slice_rows = block_rows // lax.axis_size("src")
    panel = lax.all_to_all(ordered, "src", split_axis=0, concat_axis=2, tiled=True)
    shot_count = panel.shape[2]
    base = panel.astype(jnp.float32)
    wave_real = wavelet_inverse[0]
    wave_imag = wavelet_inverse[1]
    real_data = slice_data[0].reshape(block_rows, -1)
    imag_data = slice_data[1].reshape(block_rows, -1)
    estimate = panel
    predicted = jnp.zeros((slice_rows, 2, shot_count), jnp.float32)
    primaries = base
    for iteration in range(ITERS):
        shard_rows = lax.all_gather(estimate, "row", axis=0, tiled=True)
        piece_rows = shard_rows.shape[0]
        stacked = shard_rows.reshape(piece_rows, 2 * shot_count)
        real_terms = jnp.dot(real_data, stacked, preferred_element_type=jnp.float32)
        imag_terms = jnp.dot(imag_data, stacked, preferred_element_type=jnp.float32)
        summed = lax.psum(combine_parts(real_terms, imag_terms, shot_count), "src")
        predicted = lax.dynamic_slice_in_dim(
            summed, lax.axis_index("src") * slice_rows, slice_rows, 0
        )
        next_real = base[:, 0] - (wave_real * predicted[:, 0] - wave_imag * predicted[:, 1])
        next_imag = base[:, 1] - (wave_real * predicted[:, 1] + wave_imag * predicted[:, 0])
        primaries = jnp.stack([next_real, next_imag], axis=1)
        estimate = primaries.astype(jnp.bfloat16)
    return (predicted, primaries)


def solution(mesh):
    in_specs = (P("row", "src", None), P("row"), P(None, "row", None, "src"), P())
    out_specs = (P(("row", "src"), None, None), P(("row", "src"), None, None))
    return jax.shard_map(body, mesh=mesh, in_specs=in_specs, out_specs=out_specs, check_vma=False)
```

profile of v0, /device:TPU:2, one launch (start us, length us, event | category | flops | bytes accessed | tf_op | source)
XLA Modules:
  0.0 753.8 jit_solution(3112653908474504425)
XLA Ops:
  7.2 0.1 multiply_convert_fusion
  7.3 0.0 copy-start
  7.3 5.6 fusion
  12.9 0.2 convert_element_type.54
  13.2 0.3 copy.48
  13.5 0.9 reshape.153
  14.3 9.0 %all-to-all-start = ((bf16[32,2,256]{2,1,0:T(2,128)(2,1)}), bf16[32,2,256]{2,1,0:T(2,128)(2,1)S(1)}, u32[]{:S(2)}, u32[]{:S(2)}) async-start(bf16[32,2,256]{2,1,0:T(2,128)(2,1)} %reshape.153), calls=%async_computation | async-start | bytes 65536 | tf_op jit(solution)/shard_map/all_to_all | solution.py:43
  23.3 0.0 all-gather.4.cloned.1.call-start
  23.4 0.0 copy-done
  23.4 7.0 all-to-all-done
  30.4 0.2 reshape.154
  30.6 2.1 gather_fusion
  32.7 0.3 reshape.155
  33.0 15.2 %all_to_all.23 = bf16[8,2,1024]{2,1,0:T(2,128)(2,1)S(1)} all-to-all(bf16[8,2,1024]{2,1,0:T(2,128)(2,1)S(1)} %reshape.155), channel_id=1, replica_groups=mesh['row'=32,'src'=8] {'src'}, dimensions={0} | all-to-all | bytes 65536 | tf_op jit(solution)/shard_map/all_to_all | solution.py:48
  48.3 0.2 reshape.156
  48.5 0.2 copy.14
  48.6 0.7 copy.15
  49.4 0.0 all-gather.4.cloned.1.call-update
  49.4 0.0 all-reduce.4.cloned.1.call-start
  49.4 4.0 fusion.41
  53.4 136.0 %all-gather.4.cloned.1.call-done = bf16[2048,2,128]{2,1,0:T(2,128)(2,1)} async-done(((bf16[64,2,128]{2,1,0:T(2,128)(2,1)}), bf16[2048,2,128]{2,1,0:T(2,128)(2,1)}) %all-gather.4.cloned.1.call-update) | async-done | bytes 1048592 | tf_op jit(solution)/shard_map/all_gather | solution.py:59
  189.4 0.0 copy-start.2
  189.4 2.7 convolution_bitcast_fusion.4
  192.1 0.0 copy-done.2
  192.1 0.7 convolution_bitcast_fusion.5
  192.9 0.0 copy-start.1
  192.9 0.1 fusion.18
  193.0 0.8 pad_maximum_fusion
  193.8 0.0 all-reduce.4.cloned.1.call-update
  193.9 0.0 all-gather.6.cloned.1.call-start
  193.9 0.0 copy-done.1
  193.9 0.6 fusion.42
  194.5 80.9 %all-reduce.4.cloned.1.call-done = f32[512,2,128]{0,2,1:T(8,128)} async-done(((f32[512,2,128]{0,2,1:T(8,128)}), f32[512,2,128]{0,2,1:T(8,128)}) %all-reduce.4.cloned.1.call-update) | async-done | bytes 524304 | tf_op jit(solution)/shard_map/psum | solution.py:64
  275.5 2.1 subtract_convert_fusion.3
  277.6 0.7 copy.16
  278.4 0.0 all-gather.6.cloned.1.call-update
  278.4 0.0 all-reduce.6.cloned.1.call-start
  278.4 144.4 %all-gather.6.cloned.1.call-done = bf16[2048,2,128]{2,1,0:T(2,128)(2,1)} async-done(((bf16[64,2,128]{2,1,0:T(2,128)(2,1)}), bf16[2048,2,128]{2,1,0:T(2,128)(2,1)}) %all-gather.6.cloned.1.call-update) | async-done | bytes 1048592 | tf_op jit(solution)/shard_map/all_gather | solution.py:59
  422.9 0.0 copy-start.4
  422.9 2.7 convolution_bitcast_fusion.2
  425.6 0.0 copy-done.4
  425.6 0.7 convolution_bitcast_fusion.3
  426.4 0.1 fusion.16
  426.5 0.8 pad_maximum_fusion.1
  427.3 0.0 all-reduce.6.cloned.1.call-update
  427.3 0.0 all-gather.8.cloned.1.call-start
  427.4 81.5 %all-reduce.6.cloned.1.call-done = f32[512,2,128]{0,2,1:T(8,128)} async-done(((f32[512,2,128]{0,2,1:T(8,128)}), f32[512,2,128]{0,2,1:T(8,128)}) %all-reduce.6.cloned.1.call-update) | async-done | bytes 524304 | tf_op jit(solution)/shard_map/psum | solution.py:64
  508.8 2.1 subtract_convert_fusion.1
  511.0 0.7 copy.17
  511.7 0.0 all-gather.8.cloned.1.call-update
  511.8 0.0 all-reduce.8.cloned.1.call-start
  511.8 144.4 %all-gather.8.cloned.1.call-done = bf16[2048,2,128]{2,1,0:T(2,128)(2,1)} async-done(((bf16[64,2,128]{2,1,0:T(2,128)(2,1)}), bf16[2048,2,128]{2,1,0:T(2,128)(2,1)}) %all-gather.8.cloned.1.call-update) | async-done | bytes 1048592 | tf_op jit(solution)/shard_map/all_gather | solution.py:59
  656.3 0.0 copy-start.3
  656.3 2.7 convolution_bitcast_fusion
  659.0 0.0 copy-done.3
  659.0 0.7 convolution_bitcast_fusion.1
  659.8 0.1 fusion.14
  659.8 0.8 pad_maximum_fusion.2
  660.7 0.0 all-reduce.8.cloned.1.call-update
  660.7 81.6 %all-reduce.8.cloned.1.call-done = f32[512,2,128]{0,2,1:T(8,128)} async-done(((f32[512,2,128]{0,2,1:T(8,128)}), f32[512,2,128]{0,2,1:T(8,128)}) %all-reduce.8.cloned.1.call-update) | async-done | bytes 524304 | tf_op jit(solution)/shard_map/psum | solution.py:64
  742.3 1.0 constant_dynamic-slice_fusion
  743.3 0.7 copy.18
  744.0 2.1 subtract_subtract_fusion
  746.2 0.7 copy.19
  (6 shorter events, 0.1 us)
Async XLA Ops:
  7.3 16.1 %copy-start = (s32[512]{0:T(512)S(1)}, s32[512]{0:T(512)}, u32[]{:S(2)}) copy-start(s32[512]{0:T(512)} %param.5) | copy-start | bytes 6148
  14.3 16.1 %all-to-all-start = ((bf16[32,2,256]{2,1,0:T(2,128)(2,1)}), bf16[32,2,256]{2,1,0:T(2,128)(2,1)S(1)}, u32[]{:S(2)}, u32[]{:S(2)}) async-start(bf16[32,2,256]{2,1,0:T(2,128)(2,1)} %reshape.153), calls=%async_computation | async-start | bytes 65536 | tf_op jit(solution)/shard_map/all_to_all | solution.py:43
  23.3 166.1 %all-gather.4.cloned.1.call-start = ((), (), s32[]{:S(2)}) async-start(), calls=%async_computation.2 | async-start | bytes 1081344 | tf_op jit(solution)/shard_map/all_gather | solution.py:59
  49.4 226.1 %all-reduce.4.cloned.1.call-start = ((), (), s32[]{:S(2)}) async-start(), calls=%async_computation.3 | async-start | bytes 1048576 | tf_op jit(solution)/shard_map/psum | solution.py:64
  189.4 2.7 copy-start.2
  192.9 1.0 copy-start.1
  193.9 229.0 %all-gather.6.cloned.1.call-start = ((), (), s32[]{:S(2)}) async-start(), calls=%async_computation.4 | async-start | bytes 1081344 | tf_op jit(solution)/shard_map/all_gather | solution.py:59
  278.4 230.5 %all-reduce.6.cloned.1.call-start = ((), (), s32[]{:S(2)}) async-start(), calls=%async_computation.5 | async-start | bytes 1048576 | tf_op jit(solution)/shard_map/psum | solution.py:64
  422.9 2.7 copy-start.4
  427.3 229.0 %all-gather.8.cloned.1.call-start = ((), (), s32[]{:S(2)}) async-start(), calls=%async_computation.6 | async-start | bytes 1081344 | tf_op jit(solution)/shard_map/all_gather | solution.py:59
  511.8 230.6 %all-reduce.8.cloned.1.call-start = ((), (), s32[]{:S(2)}) async-start(), calls=%async_computation.7 | async-start | bytes 1048576 | tf_op jit(solution)/shard_map/psum | solution.py:64
  656.3 2.7 copy-start.3
Sparse Core Ops, SparseCore 0:
  49.5 139.8 all-gather.3
  194.0 81.4 all-reduce.3
  278.5 144.3 all-gather.5
  427.4 81.3 all-reduce.5
  511.9 144.3 all-gather.7
  660.8 81.4 all-reduce.7
where the time goes:
time: 754 us
  waiting for transfers between devices  676 us (90%)
  matrix products  16 us (2%)
  blocking collectives  15.2 us (2%)
  between operations  14.4 us (2%)
  local copies, waits for them, and re-layouts  13.5 us (2%)
  other arithmetic  9.38 us (1%)
  starting transfers between devices  9.22 us (1%)
    all_gather x3, waiting for transfers between devices, body(): shard_rows = lax.all_gather(estimate, 'row', axis=0, tiled=True)  425 us
    psum x3, waiting for transfers between devices, body(): summed = lax.psum(combine_parts(real_terms, imag_terms, shot_count), 'src')  244 us
    all_to_all x1, blocking collectives, body(): lax.all_to_all(ordered, 'src', split_axis=0, concat_axis=2, tiled=True)  15.2 us
  transfers between devices with their start and end apart: 7, of which 7 were waited for; matrix products, arithmetic and copies ran while one was open for 1% of the time, Pallas kernels for 0%

commit v1 on v0

--- a/solution.py
+++ b/solution.py
@@ -61,7 +61,9 @@
         stacked = shard_rows.reshape(piece_rows, 2 * shot_count)
         real_terms = jnp.dot(real_data, stacked, preferred_element_type=jnp.float32)
         imag_terms = jnp.dot(imag_data, stacked, preferred_element_type=jnp.float32)
-        summed = lax.psum(combine_parts(real_terms, imag_terms, shot_count), "src")
+        summed = jnp.sum(
+            lax.all_gather(combine_parts(real_terms, imag_terms, shot_count), "src"), 0
+        )
         predicted = lax.dynamic_slice_in_dim(
             summed, lax.axis_index("src") * slice_rows, slice_rows, 0
         )

time: 754 us -> 722 us (0.958)
  waiting for transfers between devices: 676 us -> 611 us
  local copies, waits for them, and re-layouts: 13.5 us -> 36.7 us
    psum x3 -> x0, waiting for transfers between devices: 244 us -> none  [body(): summed = lax.psum(combine_parts(real_terms, imag_terms, shot_count), 'src')]
    all_gather x0 -> x3, waiting for transfers between devices: none -> 177 us  [body(): lax.all_gather(combine_parts(real_terms, imag_terms, shot_count), 'src')]
    unnamed x16 -> x19, local copies, waits for them, and re-layouts: 3.02 us -> 27 us
    reduce_sum x0 -> x3, other arithmetic: none -> 9.56 us  [body(): jnp.sum(lax.all_gather(combine_parts(real_terms, imag_terms, shot_count),...]
where the time goes in v1:
time: 722 us; the launch traced here: 719 us
  waiting for transfers between devices  611 us (85%)
  local copies, waits for them, and re-layouts  36.7 us (5%)
  other arithmetic  16.8 us (2%)
  matrix products  16 us (2%)
  blocking collectives  15.2 us (2%)
  between operations  14.4 us (2%)
  starting transfers between devices  9.62 us (1%)
    all_gather x3, waiting for transfers between devices, body(): shard_rows = lax.all_gather(estimate, 'row', axis=0, tiled=True)  426 us
    all_gather x3, waiting for transfers between devices, body(): lax.all_gather(combine_parts(real_terms, imag_terms, shot_count), 'src')  177 us
    unnamed x19, local copies, waits for them, and re-layouts  27 us
    all_to_all x1, blocking collectives, body(): lax.all_to_all(ordered, 'src', split_axis=0, concat_axis=2, tiled=True)  15.2 us
  transfers between devices with their start and end apart: 7, of which 7 were waited for; matrix products, arithmetic and copies ran while one was open for 1% of the time, Pallas kernels for 0%

profile of v1, /device:TPU:2, one launch (start us, length us, event | category | flops | bytes accessed | tf_op | source)
XLA Modules:
  0.0 719.3 jit_solution(4921269796708357343)
XLA Ops:
  7.2 0.1 multiply_convert_fusion
  7.3 0.0 copy-start
  7.3 5.6 fusion
  12.9 0.2 convert_element_type.54
  13.2 0.3 copy.52
  13.5 0.9 reshape.156
  14.3 9.0 %all-to-all-start = ((bf16[32,2,256]{2,1,0:T(2,128)(2,1)}), bf16[32,2,256]{2,1,0:T(2,128)(2,1)S(1)}, u32[]{:S(2)}, u32[]{:S(2)}) async-start(bf16[32,2,256]{2,1,0:T(2,128)(2,1)} %reshape.156), calls=%async_computation | async-start | bytes 65536 | tf_op jit(solution)/shard_map/all_to_all | solution.py:43
  23.3 0.0 all-gather.10.cloned.1.call-start
  23.4 0.0 copy-done
  23.4 7.0 all-to-all-done
  30.4 0.2 reshape.157
  30.6 2.1 gather_fusion
  32.7 0.3 reshape.158
  33.0 15.2 %all_to_all.23 = bf16[8,2,1024]{2,1,0:T(2,128)(2,1)S(1)} all-to-all(bf16[8,2,1024]{2,1,0:T(2,128)(2,1)S(1)} %reshape.158), channel_id=1, replica_groups=mesh['row'=32,'src'=8] {'src'}, dimensions={0} | all-to-all | bytes 65536 | tf_op jit(solution)/shard_map/all_to_all | solution.py:48
  48.3 0.2 reshape.159
  48.5 0.2 copy.12
  48.6 0.7 copy.13
  49.4 0.0 all-gather.10.cloned.1.call-update
  49.4 0.0 all-gather.16.cloned.1.call-start
  49.4 4.0 fusion.41
  53.5 135.9 %all-gather.10.cloned.1.call-done = bf16[2048,2,128]{2,1,0:T(2,128)(2,1)} async-done(((bf16[64,2,128]{2,1,0:T(2,128)(2,1)}), bf16[2048,2,128]{2,1,0:T(2,128)(2,1)}) %all-gather.10.cloned.1.call-update) | async-done | bytes 1048592 | tf_op jit(solution)/shard_map/all_gather | solution.py:59
  189.4 2.7 convolution_bitcast_fusion.4
  192.1 0.0 copy-done.2
  192.2 0.7 convolution_bitcast_fusion.5
  192.9 0.0 copy-start.1
  192.9 0.1 fusion.18
  193.0 0.8 pad_maximum_fusion
  193.8 0.0 all-gather.16.cloned.1.call-update
  193.9 0.0 all-gather.12.cloned.1.call-start
  193.9 0.7 fusion.42
  194.6 58.5 %all-gather.16.cloned.1.call-done = f32[4096,2,128]{0,2,1:T(8,128)} async-done(((f32[512,2,128]{0,2,1:T(8,128)}), f32[4096,2,128]{0,2,1:T(8,128)}) %all-gather.16.cloned.1.call-update) | async-done | bytes 4194320 | tf_op jit(solution)/shard_map/all_gather | solution.py:65
  253.1 8.0 %copy.19 = f32[32,8,8,512]{3,2,1,0:T(8,128)} copy(f32[32,8,8,512]{3,1,2,0:T(8,128)} %bitcast.88) | data formatting | bytes 8388608
  261.1 3.2 reduce_sum.27
  264.3 1.4 subtract_convert_fusion.3
  265.8 0.7 copy.14
  266.5 0.0 all-gather.12.cloned.1.call-update
  266.5 0.2 all-gather.18.cloned.1.call-start
  266.8 145.2 %all-gather.12.cloned.1.call-done = bf16[2048,2,128]{2,1,0:T(2,128)(2,1)} async-done(((bf16[64,2,128]{2,1,0:T(2,128)(2,1)}), bf16[2048,2,128]{2,1,0:T(2,128)(2,1)}) %all-gather.12.cloned.1.call-update) | async-done | bytes 1048592 | tf_op jit(solution)/shard_map/all_gather | solution.py:59
  412.0 2.7 convolution_bitcast_fusion.2
  414.7 0.7 convolution_bitcast_fusion.3
  415.5 0.1 fusion.16
  415.6 0.8 pad_maximum_fusion.1
  416.4 0.0 all-gather.18.cloned.1.call-update
  416.4 0.0 all-gather.14.cloned.1.call-start
  416.5 59.3 %all-gather.18.cloned.1.call-done = f32[4096,2,128]{0,2,1:T(8,128)} async-done(((f32[512,2,128]{0,2,1:T(8,128)}), f32[4096,2,128]{0,2,1:T(8,128)}) %all-gather.18.cloned.1.call-update) | async-done | bytes 4194320 | tf_op jit(solution)/shard_map/all_gather | solution.py:65
  475.7 8.0 %copy.21 = f32[32,8,8,512]{3,2,1,0:T(8,128)} copy(f32[32,8,8,512]{3,1,2,0:T(8,128)} %bitcast.89) | data formatting | bytes 8388608
  483.7 3.2 reduce_sum.28
  486.9 1.4 subtract_convert_fusion.1
  488.4 0.7 copy.15
  489.1 0.0 all-gather.14.cloned.1.call-update
  489.1 0.3 all-gather.20.cloned.1.call-start
  489.4 145.2 %all-gather.14.cloned.1.call-done = bf16[2048,2,128]{2,1,0:T(2,128)(2,1)} async-done(((bf16[64,2,128]{2,1,0:T(2,128)(2,1)}), bf16[2048,2,128]{2,1,0:T(2,128)(2,1)}) %all-gather.14.cloned.1.call-update) | async-done | bytes 1048592 | tf_op jit(solution)/shard_map/all_gather | solution.py:59
  634.6 2.7 convolution_bitcast_fusion
  637.3 0.7 convolution_bitcast_fusion.1
  638.1 0.1 fusion.14
  638.2 0.8 pad_maximum_fusion.2
  639.0 0.0 all-gather.20.cloned.1.call-update
  639.0 59.3 %all-gather.20.cloned.1.call-done = f32[4096,2,128]{0,2,1:T(8,128)} async-done(((f32[512,2,128]{0,2,1:T(8,128)}), f32[4096,2,128]{0,2,1:T(8,128)}) %all-gather.20.cloned.1.call-update) | async-done | bytes 4194320 | tf_op jit(solution)/shard_map/all_gather | solution.py:65
  698.3 8.0 %copy.23 = f32[32,8,8,512]{3,2,1,0:T(8,128)} copy(f32[32,8,8,512]{3,1,2,0:T(8,128)} %bitcast.90) | data formatting | bytes 8388608
  706.3 3.2 reduce_sum.29
  709.5 1.4 subtract_subtract_fusion
  710.9 0.1 constant_dynamic-slice_fusion
  711.1 0.7 copy.16
  711.8 0.7 copy.17
  (12 shorter events, 0.1 us)
Async XLA Ops:
  7.3 16.1 %copy-start = (s32[512]{0:T(512)S(1)}, s32[512]{0:T(512)}, u32[]{:S(2)}) copy-start(s32[512]{0:T(512)} %param.5) | copy-start | bytes 6148
  14.3 16.1 %all-to-all-start = ((bf16[32,2,256]{2,1,0:T(2,128)(2,1)}), bf16[32,2,256]{2,1,0:T(2,128)(2,1)S(1)}, u32[]{:S(2)}, u32[]{:S(2)}) async-start(bf16[32,2,256]{2,1,0:T(2,128)(2,1)} %reshape.156), calls=%async_computation | async-start | bytes 65536 | tf_op jit(solution)/shard_map/all_to_all | solution.py:43
  23.3 166.1 %all-gather.10.cloned.1.call-start = ((), (), s32[]{:S(2)}) async-start(), calls=%async_computation.2 | async-start | bytes 1081344 | tf_op jit(solution)/shard_map/all_gather | solution.py:59
  49.4 203.8 %all-gather.16.cloned.1.call-start = ((), (), s32[]{:S(2)}) async-start(), calls=%async_computation.5 | async-start | bytes 4718592 | tf_op jit(solution)/shard_map/all_gather | solution.py:65
  189.4 2.7 copy-start.2
  192.9 1.0 copy-start.1
  193.9 218.1 %all-gather.12.cloned.1.call-start = ((), (), s32[]{:S(2)}) async-start(), calls=%async_computation.3 | async-start | bytes 1081344 | tf_op jit(solution)/shard_map/all_gather | solution.py:59
  266.5 209.2 %all-gather.18.cloned.1.call-start = ((), (), s32[]{:S(2)}) async-start(), calls=%async_computation.6 | async-start | bytes 4718592 | tf_op jit(solution)/shard_map/all_gather | solution.py:65
  412.0 2.7 copy-start.4
  416.4 218.2 %all-gather.14.cloned.1.call-start = ((), (), s32[]{:S(2)}) async-start(), calls=%async_computation.4 | async-start | bytes 1081344 | tf_op jit(solution)/shard_map/all_gather | solution.py:59
  489.1 209.2 %all-gather.20.cloned.1.call-start = ((), (), s32[]{:S(2)}) async-start(), calls=%async_computation.7 | async-start | bytes 4718592 | tf_op jit(solution)/shard_map/all_gather | solution.py:65
  634.6 2.7 copy-start.3
Sparse Core Ops, SparseCore 0:
  49.5 139.8 all-gather.9
  194.0 59.1 all-gather.15
  266.7 145.2 all-gather.11
  416.5 59.1 all-gather.17
  489.3 145.2 all-gather.13
  639.2 59.1 all-gather.19
